TPU v7x, 512 devices: a whole 4x4x16 slice. The times are simulated.
512 devices in a mesh: wide: 32 (over x_lo, z), grp: 16 (over y, x_hi, core).
Axes of the slice: x: 4 (x_hi: 2, x_lo: 2; x = x_hi * 2 + x_lo), y: 4, z: 16, core: 2. Of those that a mesh axis runs over, the one named last changes fastest.
Arguments:
- log_hazards: float32 [25, 25], replicated, may hold values from -0.5 to 0.5
- bit_order: int32 [25], replicated, may hold values from 0 to 24, each once
- patients: int32 [256], replicated, may hold values from 0 to 33554431, as said below
- start_dist: float32 [33554432], P(('wide', 'grp')), may hold values from 0.25 to 4
- start_adjoint: float32 [33554432], P(('wide', 'grp')), may hold values from -6 to 6
Outputs:
- distribution: float32 [33554432], P(('wide', 'grp'))
- loglik: float32 [], replicated
- gradient: float32 [25, 25], replicated
- empty_state: float32 [], replicated
Inputs may be any that keep to these rules, and one draw needn't show every extreme that they name: `patients`: each value is a set of events, bit e set when event e is present; every draw has a patient with no event and one with all 25. `bit_order`: A permutation of the events.
All inputs are finite; a program needn't handle non-finite values.
Results may differ from a plain program's by a relative error of at most 0.0003.
Values sent between devices are 32-bit elements; how exact they have to be, the bound alone decides.
A program may use at most 64 MiB of HBM per device.

v0:
```python
import jax
import jax.numpy as jnp
import numpy as np
from jax import lax
from jax.sharding import PartitionSpec as P

highest = lax.Precision.HIGHEST


def partner_2(value, axis, distance):
    mask = 2**distance
    pairs = [(source, source ^ mask) for source in range(lax.axis_size(axis))]
    return lax.ppermute(value, axis, pairs)


def bit_table(number, columns):
    positions = jnp.arange(number, dtype=jnp.int32)
    shifts = jnp.arange(columns, dtype=jnp.int32)
    return (positions[:, None] >> shifts[None, :] & 1).astype(jnp.float32)


def index_bits(position, columns):
    shifts = jnp.arange(columns, dtype=jnp.int32)
    return (position >> shifts & 1).astype(jnp.float32)


def pick_columns(matrix, ranges):
    return jnp.concatenate(
        [matrix[:, begin_at : begin_at + length] for begin_at, length in ranges], axis=1
    )


def order_table(ranges, count_bits):
    listed = [begin_at + offset for begin_at, length in ranges for offset in range(length)]
    table = np.zeros((count_bits, count_bits), np.float32)
    table[np.arange(count_bits), np.array(listed, np.int64)] = 1.0
    return jnp.asarray(table)


def lane_tables(lane_bits_count, lane_count):
    source = jnp.arange(lane_count, dtype=jnp.int32)
    blocks = []
    for lane_bit in range(lane_bits_count):
        stride = 2**lane_bit
        lower_half = source >> lane_bit & 1 == 0
        blocks.append(
            ((source[None, :] == source[:, None] + stride) & lower_half[:, None]).astype(
                jnp.float32
            )
        )
    return jnp.concatenate(blocks, axis=0)


def rate_maker(coupling, diagonal, layout, row_bits, lane_bits):
    row_ranges, lane_ranges, device_ranges, device_values, block_begin, block_count = layout
    block_rows = coupling[block_begin : block_begin + block_count]
    offsets = diagonal[block_begin : block_begin + block_count] + jnp.dot(
        pick_columns(block_rows, device_ranges), device_values, precision=highest
    )
    by_row = jnp.dot(row_bits, pick_columns(block_rows, row_ranges).T, precision=highest)
    by_lane = jnp.dot(lane_bits, pick_columns(block_rows, lane_ranges).T, precision=highest)

    def rate_of(position):
        return jnp.exp(
            offsets[position] + by_row[:, position][:, None] + by_lane[:, position][None, :]
        )

    return rate_of


def row_split(values, row_bit):
    row_count, lane_count = values.shape
    return values.reshape(row_count >> row_bit + 1, 2, 2**row_bit, lane_count)


def join_rows(lower_half, upper_half):
    paired = jnp.stack([lower_half, upper_half], axis=1)
    return paired.reshape(-1, paired.shape[-1])


def local_push(values, rate_of, lane_part, row_start, block_count, lane_push):
    summed = jnp.zeros_like(values)
    if lane_part > 0:
        stacked = jnp.concatenate(
            [rate_of(position) * values for position in range(lane_part)], axis=1
        )
        summed = jnp.dot(stacked, lane_push, precision=highest)
    for position in range(lane_part, block_count):
        moving = row_split(rate_of(position) * values, row_start + position - lane_part)
        summed = summed + join_rows(jnp.zeros_like(moving[:, 0]), moving[:, 0])
    return summed


def local_pull(values, rate_of, lane_part, row_start, block_count, lane_pull):
    summed = jnp.zeros_like(values)
    lane_count = values.shape[1]
    if lane_part > 0:
        partners = jnp.dot(values, lane_pull, precision=highest)
        for position in range(lane_part):
            summed = (
                summed
                + rate_of(position)
                * partners[:, position * lane_count : (position + 1) * lane_count]
            )
    for position in range(lane_part, block_count):
        row_bit = row_start + position - lane_part
        others = row_split(values, row_bit)
        rates = row_split(rate_of(position), row_bit)
        summed = summed + join_rows(rates[:, 0] * others[:, 1], jnp.zeros_like(others[:, 1]))
    return summed


def local_gradient(
    forward, adjoint, rate_of, lane_part, row_start, block_count, lane_pull, lane_low
):
    contribs = []
    lane_count = forward.shape[1]
    if lane_part > 0:
        partners = jnp.dot(adjoint, lane_pull, precision=highest)
        for position in range(lane_part):
            partner = partners[:, position * lane_count : (position + 1) * lane_count]
            contribs.append(
                rate_of(position) * forward * (partner - adjoint) * lane_low[position][None, :]
            )
    for position in range(lane_part, block_count):
        row_bit = row_start + position - lane_part
        others = row_split(adjoint, row_bit)
        rates = row_split(rate_of(position), row_bit)
        forwards = row_split(forward, row_bit)
        lower_term = rates[:, 0] * forwards[:, 0] * (others[:, 1] - others[:, 0])
        contribs.append(join_rows(lower_term, jnp.zeros_like(lower_term)))
    return contribs


def feature_row(contrib, row_bits, lane_bits, device_values, to_global, own_bit):
    per_row = jnp.sum(contrib, axis=1)
    per_lane = jnp.sum(contrib, axis=0)
    whole = jnp.sum(per_row)
    listed = jnp.concatenate(
        [
            jnp.dot(per_row, row_bits, precision=highest),
            jnp.dot(per_lane, lane_bits, precision=highest),
            whole * device_values,
        ]
    )
    own_column = (jnp.arange(to_global.shape[0], dtype=jnp.int32) == own_bit).astype(jnp.float32)
    return jnp.dot(listed, to_global, precision=highest) + whole * own_column


def body(log_hazards, bit_order, patients, start_dist, start_adjoint):
    count_bits = log_hazards.shape[0]
    local_count = start_dist.shape[0]
    patient_count = patients.shape[0]
    wide_count = lax.axis_size("wide")
    grp_count = lax.axis_size("grp")
    wide_bits = wide_count.bit_length() - 1
    grp_bits = grp_count.bit_length() - 1
    local_bits = local_count.bit_length() - 1
    lane_bits_count = min(7, local_bits - wide_bits - grp_bits)
    lane_count = 2**lane_bits_count
    row_count = local_count // lane_count
    row_bits_count = local_bits - lane_bits_count
    wide_index = lax.axis_index("wide")
    grp_index = lax.axis_index("grp")
    wide_values = index_bits(wide_index, wide_bits)
    grp_values = index_bits(grp_index, grp_bits)
    device_values = jnp.concatenate([grp_values, wide_values])
    shifts = jnp.arange(count_bits, dtype=jnp.int32)
    onehot = (bit_order[:, None] == shifts[None, :]).astype(jnp.float32)
    by_bits = jnp.dot(onehot.T, jnp.dot(log_hazards, onehot, precision=highest), precision=highest)
    diagonal = jnp.diagonal(by_bits)
    coupling = by_bits * (1.0 - jnp.eye(count_bits, dtype=jnp.float32))
    row_bits = bit_table(row_count, row_bits_count)
    lane_bits = bit_table(lane_count, lane_bits_count)
    lane_push = lane_tables(lane_bits_count, lane_count)
    lane_pull = lane_push.T
    lane_low = 1.0 - lane_bits.T
    home_rows = [(lane_bits_count, row_bits_count)]
    lane_ranges = [(0, lane_bits_count)]
    home_devices = [(local_bits, grp_bits), (local_bits + grp_bits, wide_bits)]
    home_rate = rate_maker(
        coupling,
        diagonal,
        (home_rows, lane_ranges, home_devices, device_values, 0, count_bits),
        row_bits,
        lane_bits,
    )
    home_global = order_table(home_rows + lane_ranges + home_devices, count_bits)
    away_rows = [(lane_bits_count, row_bits_count - grp_bits), (local_bits, grp_bits)]
    away_devices = [(local_bits - grp_bits, grp_bits), (local_bits + grp_bits, wide_bits)]
    away_rate = rate_maker(
        coupling,
        diagonal,
        (away_rows, lane_ranges, away_devices, device_values, local_bits, grp_bits),
        row_bits,
        lane_bits,
    )
    away_global = order_table(away_rows + lane_ranges + away_devices, count_bits)
    row_start = row_bits_count - grp_bits

    def regroup(values):
        three_way = values.reshape(grp_count, -1, lane_count)
        arrived = lax.all_to_all(three_way, "grp", split_axis=0, concat_axis=0, tiled=True)
        return arrived.reshape(row_count, lane_count)

    def wide_swap(values, wide_bit):
        return partner_2(values, "wide", wide_bit)

    denominator = jnp.ones((row_count, lane_count), jnp.float32)
    for position in range(lane_bits_count):
        denominator = denominator + home_rate(position) * lane_low[position][None, :]
    for position in range(lane_bits_count, local_bits):
        rates = row_split(home_rate(position), position - lane_bits_count)
        denominator = denominator + join_rows(rates[:, 0], jnp.zeros_like(rates[:, 0]))
    for grp_bit in range(grp_bits):
        denominator = denominator + home_rate(local_bits + grp_bit) * (1.0 - grp_values[grp_bit])
    for wide_bit in range(wide_bits):
        denominator = denominator + home_rate(local_bits + grp_bits + wide_bit) * (
            1.0 - wide_values[wide_bit]
        )
    row_iota = lax.broadcasted_iota(jnp.int32, (row_count, lane_count), 0)
    lane_iota = lax.broadcasted_iota(jnp.int32, (row_count, lane_count), 1)
    first_device = (wide_index == 0) & (grp_index == 0)
    first_state = first_device & (row_iota == 0) & (lane_iota == 0)
    source = jnp.where(first_state, float(2**count_bits), 0.0).astype(jnp.float32)
    forward = start_dist.reshape(row_count, lane_count)
    summed = source + local_push(forward, home_rate, lane_bits_count, 0, local_bits, lane_push)
    away = regroup(forward)
    summed = summed + regroup(local_push(away, away_rate, 0, row_start, grp_bits, lane_push))
    for wide_bit in range(wide_bits):
        received = wide_swap(home_rate(local_bits + grp_bits + wide_bit) * forward, wide_bit)
        summed = summed + wide_values[wide_bit] * received
    forward = summed / denominator
    present = patients[:, None] >> shifts[None, :] & 1
    state_index = jnp.sum(present << bit_order[None, :], axis=1)
    device_number = wide_index * grp_count + grp_index
    on_device = state_index >> local_bits == device_number
    local_index = jnp.where(on_device, state_index & local_count - 1, local_count)
    counts = (
        jnp.zeros((local_count,), jnp.float32)
        .at[local_index]
        .add(1.0, mode="drop")
        .reshape(row_count, lane_count)
    )
    flattened = forward.reshape(-1)
    picked = flattened[jnp.where(on_device, local_index, 0)]
    log_sum = jnp.sum(jnp.where(on_device, jnp.log(picked), 0.0))
    log_first = jnp.where(first_device, jnp.log(flattened[0]), 0.0)
    weights = counts / (patient_count * forward)
    adjoint = start_adjoint.reshape(row_count, lane_count) * 2.0 ** (-(count_bits // 2))
    summed = weights + local_pull(adjoint, home_rate, lane_bits_count, 0, local_bits, lane_pull)
    away = regroup(adjoint)
    summed = summed + regroup(local_pull(away, away_rate, 0, row_start, grp_bits, lane_pull))
    for wide_bit in range(wide_bits):
        received = wide_swap(adjoint, wide_bit)
        summed = (
            summed
            + (1.0 - wide_values[wide_bit]) * home_rate(local_bits + grp_bits + wide_bit) * received
        )
    adjoint = summed / denominator
    grad_rows = []
    home_terms = local_gradient(
        forward, adjoint, home_rate, lane_bits_count, 0, local_bits, lane_pull, lane_low
    )
    for position in range(local_bits):
        grad_rows.append(
            feature_row(
                home_terms[position], row_bits, lane_bits, device_values, home_global, position
            )
        )
    three_way = (grp_count, -1, lane_count)
    arrived = (
        lax.all_to_all(forward.reshape(three_way), "grp", split_axis=0, concat_axis=0, tiled=True),
        lax.all_to_all(adjoint.reshape(three_way), "grp", split_axis=0, concat_axis=0, tiled=True),
    )
    away_forward = arrived[0].reshape(row_count, lane_count)
    away_adjoint = arrived[1].reshape(row_count, lane_count)
    away_terms = local_gradient(
        away_forward, away_adjoint, away_rate, 0, row_start, grp_bits, lane_pull, lane_low
    )
    for position in range(grp_bits):
        grad_rows.append(
            feature_row(
                away_terms[position],
                row_bits,
                lane_bits,
                device_values,
                away_global,
                local_bits + position,
            )
        )
    for wide_bit in range(wide_bits):
        global_bit = local_bits + grp_bits + wide_bit
        received = wide_swap(adjoint, wide_bit)
        contrib = (
            (1.0 - wide_values[wide_bit]) * home_rate(global_bit) * forward * (received - adjoint)
        )
        grad_rows.append(
            feature_row(contrib, row_bits, lane_bits, device_values, home_global, global_bit)
        )
    partial_grad = jnp.stack(grad_rows)
    grad_total, log_total, empty_state = lax.psum(
        (partial_grad, log_sum, log_first), ("wide", "grp")
    )
    gradient = jnp.dot(onehot, jnp.dot(grad_total, onehot.T, precision=highest), precision=highest)
    loglik = log_total / patient_count
    distribution = jnp.where(first_state, 0.0, forward)
    return (distribution.reshape(-1), loglik, gradient, empty_state)


def solution(mesh):
    return jax.shard_map(
        body,
        mesh=mesh,
        in_specs=(P(), P(), P(), P(("wide", "grp")), P(("wide", "grp"))),
        out_specs=(P(("wide", "grp")), P(), P(), P()),
        check_vma=False,
    )
```

profile of v0, /device:TPU:1, one launch (start us, length us, event | category | flops | bytes accessed | tf_op | source)
XLA Modules:
  0.0 466.9 jit_solution(10316019383893845244)
XLA Ops:
  7.5 6.0 %fusion.490 = (f32[512]{0:T(512)S(1)}, f32[512,1]{0,1:T(1,128)}, f32[512,1]{0,1:T(1,128)S(1)}, f32[512,1]{0,1:T(1,128)S(1)}, f32[512,1]{0,1:T(1,128)S(1)}, /*ind...) fusion(f32[]{:T(128)} %broadcast.1002, f32[512,25]{0,1:T(8,128)S(1)} %fusion.133, ...), kind=kLoop, calls=%fused_computation.907 | loop fusion | flops 4096 | bytes 34852 | tf_op jit(solution)/shard_map/add | solution.py:65
  20.2 6.1 %slice_add_fusion.3 = (f32[512,1]{0,1:T(1,128)}, f32[512,1]{0,1:T(1,128)}, f32[512,1]{0,1:T(1,128)}, f32[512,1]{0,1:T(1,128)}, f32[512,1]{0,1:T(1,128)S(1)}, /*i...) fusion(f32[512,25]{0,1:T(8,128)S(1)} %fusion.133, f32[]{:T(128)} %bitcast.119, ...), kind=kLoop, calls=%fused_computation.517 | loop fusion | flops 4608 | bytes 36900 | tf_op jit(solution)/shard_map/add | solution.py:65
  29.1 4.4 collective-permute-start
  33.4 4.9 %collective-permute-start.1 = (f32[512,128]{1,0:T(8,128)}, f32[512,128]{1,0:T(8,128)}, u32[]{:S(2)}, u32[]{:S(2)}) collective-permute-start(f32[512,128]{1,0:T(8,128)} %get-tuple-element.143), channel_id=1, source_target_pairs={{0,32},{16,48},{32,0},{48,16},{64,96},{80,112},{96,64},{112,80},{1... | collective-permute-start | bytes 786440 | tf_op jit(solution)/shard_map/ppermute | solution.py:13
  38.3 8.8 %collective-permute-start.2 = (f32[512,128]{1,0:T(8,128)}, f32[512,128]{1,0:T(8,128)}, u32[]{:S(2)}, u32[]{:S(2)}) collective-permute-start(f32[512,128]{1,0:T(8,128)} %get-tuple-element.144), channel_id=1, source_target_pairs={{0,64},{16,80},{32,96},{48,112},{64,0},{80,16},{96,32},{112,48},{1... | collective-permute-start | bytes 786440 | tf_op jit(solution)/shard_map/ppermute | solution.py:13
  47.2 7.9 %collective-permute-start.3 = (f32[512,128]{1,0:T(8,128)}, f32[512,128]{1,0:T(8,128)}, u32[]{:S(2)}, u32[]{:S(2)}) collective-permute-start(f32[512,128]{1,0:T(8,128)} %get-tuple-element.145), channel_id=1, source_target_pairs={{0,128},{16,144},{32,160},{48,176},{64,192},{80,208},{96,224},{112... | collective-permute-start | bytes 786440 | tf_op jit(solution)/shard_map/ppermute | solution.py:13
  55.1 3.1 collective-permute-start.4
  59.1 8.7 %all-to-all-start.2 = ((f32[16,32,128]{2,1,0:T(8,128)}), f32[16,32,128]{2,1,0:T(8,128)S(1)}, u32[]{:S(2)}, u32[]{:S(2)}) async-start(f32[16,32,128]{2,1,0:T(8,128)} %bitcast.160), calls=%async_computation.2 | async-start | bytes 524288 | tf_op jit(solution)/shard_map/all_to_all | solution.py:203
  77.0 6.2 %fusion.483 = (f32[512]{0:T(512)S(1)}, f32[512,1]{0,1:T(1,128)}, f32[512,1]{0,1:T(1,128)}, f32[512]{0:T(512)S(1)}, f32[512,1]{0,1:T(1,128)}, /*index=5*/f32[512]...) fusion(f32[]{:T(128)} %broadcast.1002, ...), kind=kLoop, calls=%fused_computation.900 | loop fusion | flops 4096 | bytes 47140 | tf_op jit(solution)/shard_map/add | solution.py:65
  110.6 7.2 %all-to-all-start = ((f32[16,32,128]{2,1,0:T(8,128)}), f32[16,32,128]{2,1,0:T(8,128)S(1)}, u32[]{:S(2)}, u32[]{:S(2)}) async-start(f32[16,32,128]{2,1,0:T(8,128)} %bitcast.66), calls=%async_computation | async-start | bytes 524288 | tf_op jit(solution)/shard_map/all_to_all | solution.py:203
  119.9 6.6 %all-to-all-done = f32[16,32,128]{2,1,0:T(8,128)S(1)} async-done(((f32[16,32,128]{2,1,0:T(8,128)}), f32[16,32,128]{2,1,0:T(8,128)S(1)}, u32[]{:S(2)}, u32[]{:S(2)}) %all-to-all-start) | async-done | bytes 262176 | tf_op jit(solution)/shard_map/all_to_all | solution.py:203
  130.1 4.8 %all-to-all-start.3 = ((f32[16,32,128]{2,1,0:T(8,128)}), f32[16,32,128]{2,1,0:T(8,128)}, u32[]{:S(2)}, u32[]{:S(2)}) async-start(f32[16,32,128]{2,1,0:T(8,128)} %fusion.91), calls=%async_computation.3 | async-start | bytes 524288 | tf_op jit(solution)/shard_map/all_to_all | solution.py:203
  144.4 5.2 %collective-permute-start.7 = (f32[512,128]{1,0:T(8,128)}, f32[512,128]{1,0:T(8,128)}, u32[]{:S(2)}, u32[]{:S(2)}) collective-permute-start(f32[512,128]{1,0:T(8,128)} %get-tuple-element.113), channel_id=1, source_target_pairs={{0,64},{16,80},{32,96},{48,112},{64,0},{80,16},{96,32},{112,48},{1... | collective-permute-start | bytes 786440 | tf_op jit(solution)/shard_map/ppermute | solution.py:13
  153.5 9.0 %all-to-all-start.1 = ((f32[16,32,128]{2,1,0:T(8,128)}), f32[16,32,128]{2,1,0:T(8,128)}, u32[]{:S(2)}, u32[]{:S(2)}) async-start(f32[16,32,128]{2,1,0:T(8,128)} %fusion.93), calls=%async_computation.1 | async-start | bytes 524288 | tf_op jit(solution)/shard_map/all_to_all | solution.py:203
  204.8 10.6 %fusion.84 = (f32[512,128]{1,0:T(8,128)}, f32[512,128]{1,0:T(8,128)}) fusion(f32[512,128]{1,0:T(8,128)} %bitcast.870, f32[512,128]{1,0:T(8,128)} %bitcast.863, f32[512,128]{1,0:T(8,128)} %bitcast.862, f32[512,896]{1,0:T(8,128)S(1)} %fusion.414, f32[16,32,128]{2,1,0:T(8,128)} %all-to-all-done.3, f32[1,2,256,128]{3,2,1,0:T(8,128)} %stack.278, ...), kind=kOutput, calls=%fused_computation.214 | convolution fusion | flops 713555968 | bytes 12508344 | tf_op jit(solution)/shard_map/dot_general | solution.py:87
  215.5 3.2 collective-permute-start.11
  218.7 7.5 %collective-permute-start.12 = (f32[512,128]{1,0:T(8,128)}, f32[512,128]{1,0:T(8,128)}, u32[]{:S(2)}, u32[]{:S(2)}) collective-permute-start(f32[512,128]{1,0:T(8,128)} %get-tuple-element.284), channel_id=1, source_target_pairs={{0,64},{16,80},{32,96},{48,112},{64,0},{80,16},{96,32},{112,48},{1... | collective-permute-start | bytes 786440 | tf_op jit(solution)/shard_map/ppermute | solution.py:13
  226.3 8.8 %collective-permute-start.13 = (f32[512,128]{1,0:T(8,128)}, f32[512,128]{1,0:T(8,128)}, u32[]{:S(2)}, u32[]{:S(2)}) collective-permute-start(f32[512,128]{1,0:T(8,128)} %get-tuple-element.284), channel_id=1, source_target_pairs={{0,128},{16,144},{32,160},{48,176},{64,192},{80,208},{96,224},{112... | collective-permute-start | bytes 786440 | tf_op jit(solution)/shard_map/ppermute | solution.py:13
  252.1 9.2 %all-to-all-start.4 = ((f32[16,32,128]{2,1,0:T(8,128)}), f32[16,32,128]{2,1,0:T(8,128)S(1)}, u32[]{:S(2)}, u32[]{:S(2)}) async-start(f32[16,32,128]{2,1,0:T(8,128)} %bitcast.293), calls=%async_computation.4 | async-start | bytes 524288 | tf_op jit(solution)/shard_map/all_to_all | solution.py:273
  290.2 7.2 %all-to-all-start.5 = ((f32[16,32,128]{2,1,0:T(8,128)}), f32[16,32,128]{2,1,0:T(8,128)S(1)}, u32[]{:S(2)}, u32[]{:S(2)}) async-start(f32[16,32,128]{2,1,0:T(8,128)} %bitcast.295), calls=%async_computation.5 | async-start | bytes 524288 | tf_op jit(solution)/shard_map/all_to_all | solution.py:274
  302.4 3.7 all-to-all-done.5
  326.6 11.2 %broadcast_multiply_fusion.1 = (f32[9]{0:T(128)S(1)}, f32[9]{0:T(128)S(1)}, f32[9]{0:T(128)S(1)}, f32[9]{0:T(128)S(1)}, f32[9]{0:T(128)S(1)}, /*index=5*/f32[9]{...) fusion(f32[]{:T(128)} %get-tuple-element.5, ...), kind=kLoop, calls=%fused_computation.779 | loop fusion | flops 171 | bytes 756 | tf_op jit(solution)/shard_map/mul | solution.py:143
  352.8 4.5 broadcast_multiply_fusion.19
  365.1 98.9 %all-reduce.39 = (f32[]{:T(128)}, f32[25,25]{1,0:T(8,128)S(1)}, f32[]{:T(128)}) all-reduce(f32[]{:T(128)} %select_reduce_fusion, f32[25,25]{1,0:T(8,128)S(1)} %stack.321, f32[]{:T(128)S(6)} %select_n.72), channel_id=1, replica_groups=mesh['wide'=32,'grp'=16] {'wide','grp'}, use_global_device_ids=true, to_apply=%region_2.3 | all-reduce | flops 627 | bytes 5016 | tf_op jit(solution)/shard_map/psum | solution.py:302
  (566 shorter events, 201.8 us)
Async XLA Ops:
  0.7 69.5 %copy-start.43 = (f32[5]{0:T(128)}, f32[5]{0:T(128)S(1)}, u32[]{:S(2)}) copy-start(f32[5]{0:T(128)S(1)} %and_convert_fusion) | copy-start | bytes 64
  1.4 68.9 %copy-start.46 = (f32[4]{0:T(128)}, f32[4]{0:T(128)S(1)}, u32[]{:S(2)}) copy-start(f32[4]{0:T(128)S(1)} %and_convert_fusion.1) | copy-start | bytes 52
  29.1 109.6 %collective-permute-start = (f32[512,128]{1,0:T(8,128)}, f32[512,128]{1,0:T(8,128)}, u32[]{:S(2)}, u32[]{:S(2)}) collective-permute-start(f32[512,128]{1,0:T(8,128)} %get-tuple-element.142), channel_id=1, source_target_pairs={{0,16},{16,0},{32,48},{48,32},{64,80},{80,64},{96,112},{112,96},{1... | collective-permute-start | bytes 786440 | tf_op jit(solution)/shard_map/ppermute | solution.py:13
  33.4 107.9 %collective-permute-start.1 = (f32[512,128]{1,0:T(8,128)}, f32[512,128]{1,0:T(8,128)}, u32[]{:S(2)}, u32[]{:S(2)}) collective-permute-start(f32[512,128]{1,0:T(8,128)} %get-tuple-element.143), channel_id=1, source_target_pairs={{0,32},{16,48},{32,0},{48,16},{64,96},{80,112},{96,64},{112,80},{1... | collective-permute-start | bytes 786440 | tf_op jit(solution)/shard_map/ppermute | solution.py:13
  38.3 106.1 %collective-permute-start.2 = (f32[512,128]{1,0:T(8,128)}, f32[512,128]{1,0:T(8,128)}, u32[]{:S(2)}, u32[]{:S(2)}) collective-permute-start(f32[512,128]{1,0:T(8,128)} %get-tuple-element.144), channel_id=1, source_target_pairs={{0,64},{16,80},{32,96},{48,112},{64,0},{80,16},{96,32},{112,48},{1... | collective-permute-start | bytes 786440 | tf_op jit(solution)/shard_map/ppermute | solution.py:13
  47.2 102.5 %collective-permute-start.3 = (f32[512,128]{1,0:T(8,128)}, f32[512,128]{1,0:T(8,128)}, u32[]{:S(2)}, u32[]{:S(2)}) collective-permute-start(f32[512,128]{1,0:T(8,128)} %get-tuple-element.145), channel_id=1, source_target_pairs={{0,128},{16,144},{32,160},{48,176},{64,192},{80,208},{96,224},{112... | collective-permute-start | bytes 786440 | tf_op jit(solution)/shard_map/ppermute | solution.py:13
  55.1 96.5 %collective-permute-start.4 = (f32[512,128]{1,0:T(8,128)}, f32[512,128]{1,0:T(8,128)}, u32[]{:S(2)}, u32[]{:S(2)}) collective-permute-start(f32[512,128]{1,0:T(8,128)} %get-tuple-element.146), channel_id=1, source_target_pairs={{0,256},{16,272},{32,288},{48,304},{64,320},{80,336},{96,352},{112... | collective-permute-start | bytes 786440 | tf_op jit(solution)/shard_map/ppermute | solution.py:13
  59.1 51.5 %all-to-all-start.2 = ((f32[16,32,128]{2,1,0:T(8,128)}), f32[16,32,128]{2,1,0:T(8,128)S(1)}, u32[]{:S(2)}, u32[]{:S(2)}) async-start(f32[16,32,128]{2,1,0:T(8,128)} %bitcast.160), calls=%async_computation.2 | async-start | bytes 524288 | tf_op jit(solution)/shard_map/all_to_all | solution.py:203
  110.6 15.9 %all-to-all-start = ((f32[16,32,128]{2,1,0:T(8,128)}), f32[16,32,128]{2,1,0:T(8,128)S(1)}, u32[]{:S(2)}, u32[]{:S(2)}) async-start(f32[16,32,128]{2,1,0:T(8,128)} %bitcast.66), calls=%async_computation | async-start | bytes 524288 | tf_op jit(solution)/shard_map/all_to_all | solution.py:203
  130.1 23.4 %all-to-all-start.3 = ((f32[16,32,128]{2,1,0:T(8,128)}), f32[16,32,128]{2,1,0:T(8,128)}, u32[]{:S(2)}, u32[]{:S(2)}) async-start(f32[16,32,128]{2,1,0:T(8,128)} %fusion.91), calls=%async_computation.3 | async-start | bytes 524288 | tf_op jit(solution)/shard_map/all_to_all | solution.py:203
  138.7 66.0 %collective-permute-start.5 = (f32[512,128]{1,0:T(8,128)}, f32[512,128]{1,0:T(8,128)}, u32[]{:S(2)}, u32[]{:S(2)}) collective-permute-start(f32[512,128]{1,0:T(8,128)} %get-tuple-element.113), channel_id=1, source_target_pairs={{0,16},{16,0},{32,48},{48,32},{64,80},{80,64},{96,112},{112,96},{1... | collective-permute-start | bytes 786440 | tf_op jit(solution)/shard_map/ppermute | solution.py:13
  141.3 63.4 %collective-permute-start.6 = (f32[512,128]{1,0:T(8,128)}, f32[512,128]{1,0:T(8,128)}, u32[]{:S(2)}, u32[]{:S(2)}) collective-permute-start(f32[512,128]{1,0:T(8,128)} %get-tuple-element.113), channel_id=1, source_target_pairs={{0,32},{16,48},{32,0},{48,16},{64,96},{80,112},{96,64},{112,80},{1... | collective-permute-start | bytes 786440 | tf_op jit(solution)/shard_map/ppermute | solution.py:13
  144.4 60.3 %collective-permute-start.7 = (f32[512,128]{1,0:T(8,128)}, f32[512,128]{1,0:T(8,128)}, u32[]{:S(2)}, u32[]{:S(2)}) collective-permute-start(f32[512,128]{1,0:T(8,128)} %get-tuple-element.113), channel_id=1, source_target_pairs={{0,64},{16,80},{32,96},{48,112},{64,0},{80,16},{96,32},{112,48},{1... | collective-permute-start | bytes 786440 | tf_op jit(solution)/shard_map/ppermute | solution.py:13
  149.6 55.1 %collective-permute-start.8 = (f32[512,128]{1,0:T(8,128)}, f32[512,128]{1,0:T(8,128)}, u32[]{:S(2)}, u32[]{:S(2)}) collective-permute-start(f32[512,128]{1,0:T(8,128)} %get-tuple-element.113), channel_id=1, source_target_pairs={{0,128},{16,144},{32,160},{48,176},{64,192},{80,208},{96,224},{112... | collective-permute-start | bytes 786440 | tf_op jit(solution)/shard_map/ppermute | solution.py:13
  151.6 53.2 %collective-permute-start.9 = (f32[512,128]{1,0:T(8,128)}, f32[512,128]{1,0:T(8,128)}, u32[]{:S(2)}, u32[]{:S(2)}) collective-permute-start(f32[512,128]{1,0:T(8,128)} %get-tuple-element.113), channel_id=1, source_target_pairs={{0,256},{16,272},{32,288},{48,304},{64,320},{80,336},{96,352},{112... | collective-permute-start | bytes 786440 | tf_op jit(solution)/shard_map/ppermute | solution.py:13
  153.5 51.3 %all-to-all-start.1 = ((f32[16,32,128]{2,1,0:T(8,128)}), f32[16,32,128]{2,1,0:T(8,128)}, u32[]{:S(2)}, u32[]{:S(2)}) async-start(f32[16,32,128]{2,1,0:T(8,128)} %fusion.93), calls=%async_computation.1 | async-start | bytes 524288 | tf_op jit(solution)/shard_map/all_to_all | solution.py:203
  215.5 99.1 %collective-permute-start.11 = (f32[512,128]{1,0:T(8,128)}, f32[512,128]{1,0:T(8,128)}, u32[]{:S(2)}, u32[]{:S(2)}) collective-permute-start(f32[512,128]{1,0:T(8,128)} %get-tuple-element.284), channel_id=1, source_target_pairs={{0,32},{16,48},{32,0},{48,16},{64,96},{80,112},{96,64},{112,80},{1... | collective-permute-start | bytes 786440 | tf_op jit(solution)/shard_map/ppermute | solution.py:13
  218.7 95.8 %collective-permute-start.12 = (f32[512,128]{1,0:T(8,128)}, f32[512,128]{1,0:T(8,128)}, u32[]{:S(2)}, u32[]{:S(2)}) collective-permute-start(f32[512,128]{1,0:T(8,128)} %get-tuple-element.284), channel_id=1, source_target_pairs={{0,64},{16,80},{32,96},{48,112},{64,0},{80,16},{96,32},{112,48},{1... | collective-permute-start | bytes 786440 | tf_op jit(solution)/shard_map/ppermute | solution.py:13
  226.3 88.3 %collective-permute-start.13 = (f32[512,128]{1,0:T(8,128)}, f32[512,128]{1,0:T(8,128)}, u32[]{:S(2)}, u32[]{:S(2)}) collective-permute-start(f32[512,128]{1,0:T(8,128)} %get-tuple-element.284), channel_id=1, source_target_pairs={{0,128},{16,144},{32,160},{48,176},{64,192},{80,208},{96,224},{112... | collective-permute-start | bytes 786440 | tf_op jit(solution)/shard_map/ppermute | solution.py:13
  235.1 79.5 %collective-permute-start.14 = (f32[512,128]{1,0:T(8,128)}, f32[512,128]{1,0:T(8,128)}, u32[]{:S(2)}, u32[]{:S(2)}) collective-permute-start(f32[512,128]{1,0:T(8,128)} %get-tuple-element.284), channel_id=1, source_target_pairs={{0,256},{16,272},{32,288},{48,304},{64,320},{80,336},{96,352},{112... | collective-permute-start | bytes 786440 | tf_op jit(solution)/shard_map/ppermute | solution.py:13
  239.2 80.5 %collective-permute-start.10 = (f32[512,128]{1,0:T(8,128)}, f32[512,128]{1,0:T(8,128)}, u32[]{:S(2)}, u32[]{:S(2)}) collective-permute-start(f32[512,128]{1,0:T(8,128)} %get-tuple-element.284), channel_id=1, source_target_pairs={{0,16},{16,0},{32,48},{48,32},{64,80},{80,64},{96,112},{112,96},{1... | collective-permute-start | bytes 786440 | tf_op jit(solution)/shard_map/ppermute | solution.py:13
  252.1 38.1 %all-to-all-start.4 = ((f32[16,32,128]{2,1,0:T(8,128)}), f32[16,32,128]{2,1,0:T(8,128)S(1)}, u32[]{:S(2)}, u32[]{:S(2)}) async-start(f32[16,32,128]{2,1,0:T(8,128)} %bitcast.293), calls=%async_computation.4 | async-start | bytes 524288 | tf_op jit(solution)/shard_map/all_to_all | solution.py:273
  290.2 15.9 %all-to-all-start.5 = ((f32[16,32,128]{2,1,0:T(8,128)}), f32[16,32,128]{2,1,0:T(8,128)S(1)}, u32[]{:S(2)}, u32[]{:S(2)}) async-start(f32[16,32,128]{2,1,0:T(8,128)} %bitcast.295), calls=%async_computation.5 | async-start | bytes 524288 | tf_op jit(solution)/shard_map/all_to_all | solution.py:274
  321.5 142.6 %copy-start.117 = (s32[25]{0:T(128)S(1)}, s32[25]{0:T(128)}, u32[]{:S(2)}) copy-start(s32[25]{0:T(128)} %param.8) | copy-start | bytes 304
  (131 other events, 2204.8 us)
where the time goes:
time: 470 us; the launch traced here: 467 us
  starting transfers between devices  115 us (24%)
  other arithmetic  114 us (24%)
  blocking collectives  98.9 us (21%)
  matrix products  61.7 us (13%)
  local copies, waits for them, and re-layouts  56.2 us (12%)
  between operations  11 us (2%)
  waiting for transfers between devices  10.4 us (2%)
    psum x1, blocking collectives, body(): lax.psum((partial_grad, log_sum, log_first), ('wide', 'grp'))  98.9 us
    ppermute x15, starting transfers between devices, partner_2(): return lax.ppermute(value, axis, pairs)  68.5 us
    all_to_all x4, starting transfers between devices, regroup(): lax.all_to_all(three_way, 'grp', split_axis=0, concat_axis=0, tiled=True)  29.7 us
    add x4, other arithmetic, rate_of(): offsets[position] + by_row[:, position][:, None]  21.3 us
    dot_general x25, matrix products, feature_row(): return jnp.dot(listed, to_global, precision=highest) + whole * own_column  20.8 us
    another operation x26, local copies, waits for them, and re-layouts, join_rows(): paired = jnp.stack([lower_half, upper_half], axis=1)  20.4 us
    mul x13, other arithmetic, local_pull(): rates[:, 0] * others[:, 1]  18.7 us
    mul x2, other arithmetic, feature_row(): whole * device_values  15.8 us
  transfers between devices with their start and end apart: 21, of which 2 were waited for; matrix products, arithmetic and copies ran while one was open for 31% of the time, Pallas kernels for 0%

commit v1 on v0

--- a/solution.py
+++ b/solution.py
@@ -300,7 +300,7 @@
         )
     partial_grad = jnp.stack(grad_rows)
     grad_total, log_total, empty_state = lax.psum(
-        (partial_grad, log_sum, log_first), ("wide", "grp")
+        lax.psum((partial_grad, log_sum, log_first), "wide"), "grp"
     )
     gradient = jnp.dot(onehot, jnp.dot(grad_total, onehot.T, precision=highest), precision=highest)
     loglik = log_total / patient_count

time: 470 us -> 554 us (1.18)
  blocking collectives: 98.9 us -> 179 us
    psum x1 -> x2, blocking collectives: 98.9 us -> 179 us  [the longest x1 91.5 us: body(): lax.psum((partial_grad, log_sum, log_first), 'wide')]
  transfers between devices with their start and end apart: 21 -> 21, of which waited for: 2 -> 2; matrix products, arithmetic and copies ran while one was open for 31% -> 27% of each run, Pallas kernels for 0% -> 0%
where the time goes in v1:
time: 554 us; the launch traced here: 547 us
  blocking collectives  179 us (32%)
  starting transfers between devices  115 us (21%)
  other arithmetic  114 us (21%)
  matrix products  61.7 us (11%)
  local copies, waits for them, and re-layouts  56.2 us (10%)
  between operations  11 us (2%)
  waiting for transfers between devices  10.4 us (2%)
    psum x1, blocking collectives, body(): lax.psum((partial_grad, log_sum, log_first), 'wide')  91.5 us
    psum x1, blocking collectives, body(): lax.psum(lax.psum((partial_grad, log_sum, log_first), 'wide'), 'grp')  87.8 us
    ppermute x15, starting transfers between devices, partner_2(): return lax.ppermute(value, axis, pairs)  68.5 us
    all_to_all x4, starting transfers between devices, regroup(): lax.all_to_all(three_way, 'grp', split_axis=0, concat_axis=0, tiled=True)  29.7 us
    add x4, other arithmetic, rate_of(): offsets[position] + by_row[:, position][:, None]  21.3 us
    dot_general x25, matrix products, feature_row(): return jnp.dot(listed, to_global, precision=highest) + whole * own_column  20.8 us
    another operation x26, local copies, waits for them, and re-layouts, join_rows(): paired = jnp.stack([lower_half, upper_half], axis=1)  20.4 us
    mul x13, other arithmetic, local_pull(): rates[:, 0] * others[:, 1]  18.7 us
  transfers between devices with their start and end apart: 21, of which 2 were waited for; matrix products, arithmetic and copies ran while one was open for 27% of the time, Pallas kernels for 0%

profile of v1, /device:TPU:1, one launch (start us, length us, event | category | flops | bytes accessed | tf_op | source)
XLA Modules:
  0.0 547.2 jit_solution(6981198604250414685)
XLA Ops:
  7.5 6.0 %fusion.490 = (f32[512]{0:T(512)S(1)}, f32[512,1]{0,1:T(1,128)}, f32[512,1]{0,1:T(1,128)S(1)}, f32[512,1]{0,1:T(1,128)S(1)}, f32[512,1]{0,1:T(1,128)S(1)}, /*ind...) fusion(f32[]{:T(128)} %broadcast.1002, f32[512,25]{0,1:T(8,128)S(1)} %fusion.133, ...), kind=kLoop, calls=%fused_computation.907 | loop fusion | flops 4096 | bytes 34852 | tf_op jit(solution)/shard_map/add | solution.py:65
  20.2 6.1 %slice_add_fusion.3 = (f32[512,1]{0,1:T(1,128)}, f32[512,1]{0,1:T(1,128)}, f32[512,1]{0,1:T(1,128)}, f32[512,1]{0,1:T(1,128)}, f32[512,1]{0,1:T(1,128)S(1)}, /*i...) fusion(f32[512,25]{0,1:T(8,128)S(1)} %fusion.133, f32[]{:T(128)} %bitcast.119, ...), kind=kLoop, calls=%fused_computation.517 | loop fusion | flops 4608 | bytes 36900 | tf_op jit(solution)/shard_map/add | solution.py:65
  29.1 4.4 collective-permute-start
  33.4 4.9 collective-permute-start.1
  38.3 8.8 %collective-permute-start.2 = (f32[512,128]{1,0:T(8,128)}, f32[512,128]{1,0:T(8,128)}, u32[]{:S(2)}, u32[]{:S(2)}) collective-permute-start(f32[512,128]{1,0:T(8,128)} %get-tuple-element.147), channel_id=1, source_target_pairs={{0,64},{16,80},{32,96},{48,112},{64,0},{80,16},{96,32},{112,48},{1... | collective-permute-start | bytes 786440 | tf_op jit(solution)/shard_map/ppermute | solution.py:13
  47.2 7.9 %collective-permute-start.3 = (f32[512,128]{1,0:T(8,128)}, f32[512,128]{1,0:T(8,128)}, u32[]{:S(2)}, u32[]{:S(2)}) collective-permute-start(f32[512,128]{1,0:T(8,128)} %get-tuple-element.148), channel_id=1, source_target_pairs={{0,128},{16,144},{32,160},{48,176},{64,192},{80,208},{96,224},{112... | collective-permute-start | bytes 786440 | tf_op jit(solution)/shard_map/ppermute | solution.py:13
  59.1 8.7 %all-to-all-start.2 = ((f32[16,32,128]{2,1,0:T(8,128)}), f32[16,32,128]{2,1,0:T(8,128)S(1)}, u32[]{:S(2)}, u32[]{:S(2)}) async-start(f32[16,32,128]{2,1,0:T(8,128)} %bitcast.160), calls=%async_computation.2 | async-start | bytes 524288 | tf_op jit(solution)/shard_map/all_to_all | solution.py:203
  77.0 6.2 %fusion.483 = (f32[512]{0:T(512)S(1)}, f32[512,1]{0,1:T(1,128)}, f32[512,1]{0,1:T(1,128)}, f32[512]{0:T(512)S(1)}, f32[512,1]{0,1:T(1,128)}, /*index=5*/f32[512]...) fusion(f32[]{:T(128)} %broadcast.1002, ...), kind=kLoop, calls=%fused_computation.900 | loop fusion | flops 4096 | bytes 47140 | tf_op jit(solution)/shard_map/add | solution.py:65
  110.6 7.2 %all-to-all-start = ((f32[16,32,128]{2,1,0:T(8,128)}), f32[16,32,128]{2,1,0:T(8,128)S(1)}, u32[]{:S(2)}, u32[]{:S(2)}) async-start(f32[16,32,128]{2,1,0:T(8,128)} %bitcast.66), calls=%async_computation | async-start | bytes 524288 | tf_op jit(solution)/shard_map/all_to_all | solution.py:203
  119.9 6.6 %all-to-all-done = f32[16,32,128]{2,1,0:T(8,128)S(1)} async-done(((f32[16,32,128]{2,1,0:T(8,128)}), f32[16,32,128]{2,1,0:T(8,128)S(1)}, u32[]{:S(2)}, u32[]{:S(2)}) %all-to-all-start) | async-done | bytes 262176 | tf_op jit(solution)/shard_map/all_to_all | solution.py:203
  130.1 4.8 all-to-all-start.3
  144.4 5.2 collective-permute-start.7
  153.5 9.0 %all-to-all-start.1 = ((f32[16,32,128]{2,1,0:T(8,128)}), f32[16,32,128]{2,1,0:T(8,128)}, u32[]{:S(2)}, u32[]{:S(2)}) async-start(f32[16,32,128]{2,1,0:T(8,128)} %fusion.93), calls=%async_computation.1 | async-start | bytes 524288 | tf_op jit(solution)/shard_map/all_to_all | solution.py:203
  204.8 10.6 %fusion.84 = (f32[512,128]{1,0:T(8,128)}, f32[512,128]{1,0:T(8,128)}) fusion(f32[512,128]{1,0:T(8,128)} %bitcast.870, f32[512,128]{1,0:T(8,128)} %bitcast.863, f32[512,128]{1,0:T(8,128)} %bitcast.862, f32[512,896]{1,0:T(8,128)S(1)} %fusion.414, f32[16,32,128]{2,1,0:T(8,128)} %all-to-all-done.3, f32[1,2,256,128]{3,2,1,0:T(8,128)} %stack.278, ...), kind=kOutput, calls=%fused_computation.214 | convolution fusion | flops 713555968 | bytes 12508344 | tf_op jit(solution)/shard_map/dot_general | solution.py:87
  215.5 3.2 collective-permute-start.11
  218.7 7.5 %collective-permute-start.12 = (f32[512,128]{1,0:T(8,128)}, f32[512,128]{1,0:T(8,128)}, u32[]{:S(2)}, u32[]{:S(2)}) collective-permute-start(f32[512,128]{1,0:T(8,128)} %get-tuple-element.287), channel_id=1, source_target_pairs={{0,64},{16,80},{32,96},{48,112},{64,0},{80,16},{96,32},{112,48},{1... | collective-permute-start | bytes 786440 | tf_op jit(solution)/shard_map/ppermute | solution.py:13
  226.3 8.8 %collective-permute-start.13 = (f32[512,128]{1,0:T(8,128)}, f32[512,128]{1,0:T(8,128)}, u32[]{:S(2)}, u32[]{:S(2)}) collective-permute-start(f32[512,128]{1,0:T(8,128)} %get-tuple-element.287), channel_id=1, source_target_pairs={{0,128},{16,144},{32,160},{48,176},{64,192},{80,208},{96,224},{112... | collective-permute-start | bytes 786440 | tf_op jit(solution)/shard_map/ppermute | solution.py:13
  252.1 9.2 %all-to-all-start.4 = ((f32[16,32,128]{2,1,0:T(8,128)}), f32[16,32,128]{2,1,0:T(8,128)S(1)}, u32[]{:S(2)}, u32[]{:S(2)}) async-start(f32[16,32,128]{2,1,0:T(8,128)} %bitcast.293), calls=%async_computation.4 | async-start | bytes 524288 | tf_op jit(solution)/shard_map/all_to_all | solution.py:273
  290.2 7.2 %all-to-all-start.5 = ((f32[16,32,128]{2,1,0:T(8,128)}), f32[16,32,128]{2,1,0:T(8,128)S(1)}, u32[]{:S(2)}, u32[]{:S(2)}) async-start(f32[16,32,128]{2,1,0:T(8,128)} %bitcast.295), calls=%async_computation.5 | async-start | bytes 524288 | tf_op jit(solution)/shard_map/all_to_all | solution.py:274
  302.4 3.7 all-to-all-done.5
  326.6 11.2 %broadcast_multiply_fusion.1 = (f32[9]{0:T(128)S(1)}, f32[9]{0:T(128)S(1)}, f32[9]{0:T(128)S(1)}, f32[9]{0:T(128)S(1)}, f32[9]{0:T(128)S(1)}, /*index=5*/f32[9]{...) fusion(f32[]{:T(128)} %get-tuple-element.5, ...), kind=kLoop, calls=%fused_computation.779 | loop fusion | flops 171 | bytes 756 | tf_op jit(solution)/shard_map/mul | solution.py:143
  352.8 4.5 broadcast_multiply_fusion.19
  365.1 91.5 %all-reduce.39 = (f32[]{:T(128)}, f32[25,25]{1,0:T(8,128)S(1)}, f32[]{:T(128)}) all-reduce(f32[]{:T(128)} %select_reduce_fusion, f32[25,25]{1,0:T(8,128)S(1)} %stack.321, f32[]{:T(128)S(6)} %select_n.72), channel_id=1, replica_groups=mesh['wide'=32,'grp'=16] {'wide'}, use_global_device_ids=true, to_apply=%region_2.3 | all-reduce | flops 627 | bytes 5016 | tf_op jit(solution)/shard_map/psum | solution.py:303
  456.6 87.8 %all-reduce.40 = (f32[]{:T(128)}, f32[25,25]{1,0:T(8,128)S(1)}, f32[]{:T(128)}) all-reduce(f32[]{:T(128)} %get-tuple-element.82, f32[25,25]{1,0:T(8,128)S(1)} %get-tuple-element.83, f32[]{:T(128)} %get-tuple-element.84), channel_id=1, replica_groups=mesh['wide'=32,'grp'=16] {'grp'}, use_global_device_ids=true, to_apply=%region_3.4 | all-reduce | flops 627 | bytes 5016 | tf_op jit(solution)/shard_map/psum | solution.py:302
  (567 shorter events, 204.9 us)
Async XLA Ops:
  0.7 69.5 %copy-start.43 = (f32[5]{0:T(128)}, f32[5]{0:T(128)S(1)}, u32[]{:S(2)}) copy-start(f32[5]{0:T(128)S(1)} %and_convert_fusion) | copy-start | bytes 64
  1.4 68.9 %copy-start.46 = (f32[4]{0:T(128)}, f32[4]{0:T(128)S(1)}, u32[]{:S(2)}) copy-start(f32[4]{0:T(128)S(1)} %and_convert_fusion.1) | copy-start | bytes 52
  29.1 109.6 %collective-permute-start = (f32[512,128]{1,0:T(8,128)}, f32[512,128]{1,0:T(8,128)}, u32[]{:S(2)}, u32[]{:S(2)}) collective-permute-start(f32[512,128]{1,0:T(8,128)} %get-tuple-element.145), channel_id=1, source_target_pairs={{0,16},{16,0},{32,48},{48,32},{64,80},{80,64},{96,112},{112,96},{1... | collective-permute-start | bytes 786440 | tf_op jit(solution)/shard_map/ppermute | solution.py:13
  33.4 107.9 %collective-permute-start.1 = (f32[512,128]{1,0:T(8,128)}, f32[512,128]{1,0:T(8,128)}, u32[]{:S(2)}, u32[]{:S(2)}) collective-permute-start(f32[512,128]{1,0:T(8,128)} %get-tuple-element.146), channel_id=1, source_target_pairs={{0,32},{16,48},{32,0},{48,16},{64,96},{80,112},{96,64},{112,80},{1... | collective-permute-start | bytes 786440 | tf_op jit(solution)/shard_map/ppermute | solution.py:13
  38.3 106.1 %collective-permute-start.2 = (f32[512,128]{1,0:T(8,128)}, f32[512,128]{1,0:T(8,128)}, u32[]{:S(2)}, u32[]{:S(2)}) collective-permute-start(f32[512,128]{1,0:T(8,128)} %get-tuple-element.147), channel_id=1, source_target_pairs={{0,64},{16,80},{32,96},{48,112},{64,0},{80,16},{96,32},{112,48},{1... | collective-permute-start | bytes 786440 | tf_op jit(solution)/shard_map/ppermute | solution.py:13
  47.2 102.5 %collective-permute-start.3 = (f32[512,128]{1,0:T(8,128)}, f32[512,128]{1,0:T(8,128)}, u32[]{:S(2)}, u32[]{:S(2)}) collective-permute-start(f32[512,128]{1,0:T(8,128)} %get-tuple-element.148), channel_id=1, source_target_pairs={{0,128},{16,144},{32,160},{48,176},{64,192},{80,208},{96,224},{112... | collective-permute-start | bytes 786440 | tf_op jit(solution)/shard_map/ppermute | solution.py:13
  55.1 96.5 %collective-permute-start.4 = (f32[512,128]{1,0:T(8,128)}, f32[512,128]{1,0:T(8,128)}, u32[]{:S(2)}, u32[]{:S(2)}) collective-permute-start(f32[512,128]{1,0:T(8,128)} %get-tuple-element.149), channel_id=1, source_target_pairs={{0,256},{16,272},{32,288},{48,304},{64,320},{80,336},{96,352},{112... | collective-permute-start | bytes 786440 | tf_op jit(solution)/shard_map/ppermute | solution.py:13
  59.1 51.5 %all-to-all-start.2 = ((f32[16,32,128]{2,1,0:T(8,128)}), f32[16,32,128]{2,1,0:T(8,128)S(1)}, u32[]{:S(2)}, u32[]{:S(2)}) async-start(f32[16,32,128]{2,1,0:T(8,128)} %bitcast.160), calls=%async_computation.2 | async-start | bytes 524288 | tf_op jit(solution)/shard_map/all_to_all | solution.py:203
  110.6 15.9 %all-to-all-start = ((f32[16,32,128]{2,1,0:T(8,128)}), f32[16,32,128]{2,1,0:T(8,128)S(1)}, u32[]{:S(2)}, u32[]{:S(2)}) async-start(f32[16,32,128]{2,1,0:T(8,128)} %bitcast.66), calls=%async_computation | async-start | bytes 524288 | tf_op jit(solution)/shard_map/all_to_all | solution.py:203
  130.1 23.4 %all-to-all-start.3 = ((f32[16,32,128]{2,1,0:T(8,128)}), f32[16,32,128]{2,1,0:T(8,128)}, u32[]{:S(2)}, u32[]{:S(2)}) async-start(f32[16,32,128]{2,1,0:T(8,128)} %fusion.91), calls=%async_computation.3 | async-start | bytes 524288 | tf_op jit(solution)/shard_map/all_to_all | solution.py:203
  138.7 66.0 %collective-permute-start.5 = (f32[512,128]{1,0:T(8,128)}, f32[512,128]{1,0:T(8,128)}, u32[]{:S(2)}, u32[]{:S(2)}) collective-permute-start(f32[512,128]{1,0:T(8,128)} %get-tuple-element.116), channel_id=1, source_target_pairs={{0,16},{16,0},{32,48},{48,32},{64,80},{80,64},{96,112},{112,96},{1... | collective-permute-start | bytes 786440 | tf_op jit(solution)/shard_map/ppermute | solution.py:13
  141.3 63.4 %collective-permute-start.6 = (f32[512,128]{1,0:T(8,128)}, f32[512,128]{1,0:T(8,128)}, u32[]{:S(2)}, u32[]{:S(2)}) collective-permute-start(f32[512,128]{1,0:T(8,128)} %get-tuple-element.116), channel_id=1, source_target_pairs={{0,32},{16,48},{32,0},{48,16},{64,96},{80,112},{96,64},{112,80},{1... | collective-permute-start | bytes 786440 | tf_op jit(solution)/shard_map/ppermute | solution.py:13
  144.4 60.3 %collective-permute-start.7 = (f32[512,128]{1,0:T(8,128)}, f32[512,128]{1,0:T(8,128)}, u32[]{:S(2)}, u32[]{:S(2)}) collective-permute-start(f32[512,128]{1,0:T(8,128)} %get-tuple-element.116), channel_id=1, source_target_pairs={{0,64},{16,80},{32,96},{48,112},{64,0},{80,16},{96,32},{112,48},{1... | collective-permute-start | bytes 786440 | tf_op jit(solution)/shard_map/ppermute | solution.py:13
  149.6 55.1 %collective-permute-start.8 = (f32[512,128]{1,0:T(8,128)}, f32[512,128]{1,0:T(8,128)}, u32[]{:S(2)}, u32[]{:S(2)}) collective-permute-start(f32[512,128]{1,0:T(8,128)} %get-tuple-element.116), channel_id=1, source_target_pairs={{0,128},{16,144},{32,160},{48,176},{64,192},{80,208},{96,224},{112... | collective-permute-start | bytes 786440 | tf_op jit(solution)/shard_map/ppermute | solution.py:13
  151.6 53.2 %collective-permute-start.9 = (f32[512,128]{1,0:T(8,128)}, f32[512,128]{1,0:T(8,128)}, u32[]{:S(2)}, u32[]{:S(2)}) collective-permute-start(f32[512,128]{1,0:T(8,128)} %get-tuple-element.116), channel_id=1, source_target_pairs={{0,256},{16,272},{32,288},{48,304},{64,320},{80,336},{96,352},{112... | collective-permute-start | bytes 786440 | tf_op jit(solution)/shard_map/ppermute | solution.py:13
  153.5 51.3 %all-to-all-start.1 = ((f32[16,32,128]{2,1,0:T(8,128)}), f32[16,32,128]{2,1,0:T(8,128)}, u32[]{:S(2)}, u32[]{:S(2)}) async-start(f32[16,32,128]{2,1,0:T(8,128)} %fusion.93), calls=%async_computation.1 | async-start | bytes 524288 | tf_op jit(solution)/shard_map/all_to_all | solution.py:203
  215.5 99.1 %collective-permute-start.11 = (f32[512,128]{1,0:T(8,128)}, f32[512,128]{1,0:T(8,128)}, u32[]{:S(2)}, u32[]{:S(2)}) collective-permute-start(f32[512,128]{1,0:T(8,128)} %get-tuple-element.287), channel_id=1, source_target_pairs={{0,32},{16,48},{32,0},{48,16},{64,96},{80,112},{96,64},{112,80},{1... | collective-permute-start | bytes 786440 | tf_op jit(solution)/shard_map/ppermute | solution.py:13
  218.7 95.8 %collective-permute-start.12 = (f32[512,128]{1,0:T(8,128)}, f32[512,128]{1,0:T(8,128)}, u32[]{:S(2)}, u32[]{:S(2)}) collective-permute-start(f32[512,128]{1,0:T(8,128)} %get-tuple-element.287), channel_id=1, source_target_pairs={{0,64},{16,80},{32,96},{48,112},{64,0},{80,16},{96,32},{112,48},{1... | collective-permute-start | bytes 786440 | tf_op jit(solution)/shard_map/ppermute | solution.py:13
  226.3 88.3 %collective-permute-start.13 = (f32[512,128]{1,0:T(8,128)}, f32[512,128]{1,0:T(8,128)}, u32[]{:S(2)}, u32[]{:S(2)}) collective-permute-start(f32[512,128]{1,0:T(8,128)} %get-tuple-element.287), channel_id=1, source_target_pairs={{0,128},{16,144},{32,160},{48,176},{64,192},{80,208},{96,224},{112... | collective-permute-start | bytes 786440 | tf_op jit(solution)/shard_map/ppermute | solution.py:13
  235.1 79.5 %collective-permute-start.14 = (f32[512,128]{1,0:T(8,128)}, f32[512,128]{1,0:T(8,128)}, u32[]{:S(2)}, u32[]{:S(2)}) collective-permute-start(f32[512,128]{1,0:T(8,128)} %get-tuple-element.287), channel_id=1, source_target_pairs={{0,256},{16,272},{32,288},{48,304},{64,320},{80,336},{96,352},{112... | collective-permute-start | bytes 786440 | tf_op jit(solution)/shard_map/ppermute | solution.py:13
  239.2 80.5 %collective-permute-start.10 = (f32[512,128]{1,0:T(8,128)}, f32[512,128]{1,0:T(8,128)}, u32[]{:S(2)}, u32[]{:S(2)}) collective-permute-start(f32[512,128]{1,0:T(8,128)} %get-tuple-element.287), channel_id=1, source_target_pairs={{0,16},{16,0},{32,48},{48,32},{64,80},{80,64},{96,112},{112,96},{1... | collective-permute-start | bytes 786440 | tf_op jit(solution)/shard_map/ppermute | solution.py:13
  252.1 38.1 %all-to-all-start.4 = ((f32[16,32,128]{2,1,0:T(8,128)}), f32[16,32,128]{2,1,0:T(8,128)S(1)}, u32[]{:S(2)}, u32[]{:S(2)}) async-start(f32[16,32,128]{2,1,0:T(8,128)} %bitcast.293), calls=%async_computation.4 | async-start | bytes 524288 | tf_op jit(solution)/shard_map/all_to_all | solution.py:273
  290.2 15.9 %all-to-all-start.5 = ((f32[16,32,128]{2,1,0:T(8,128)}), f32[16,32,128]{2,1,0:T(8,128)S(1)}, u32[]{:S(2)}, u32[]{:S(2)}) async-start(f32[16,32,128]{2,1,0:T(8,128)} %bitcast.295), calls=%async_computation.5 | async-start | bytes 524288 | tf_op jit(solution)/shard_map/all_to_all | solution.py:274
  321.5 222.9 %copy-start.117 = (s32[25]{0:T(128)S(1)}, s32[25]{0:T(128)}, u32[]{:S(2)}) copy-start(s32[25]{0:T(128)} %param.8) | copy-start | bytes 304
  (131 other events, 2204.8 us)
